TPU v7x, 256 devices: a whole 4x4x8 slice. The times are simulated.
256 devices in a mesh: dp: 32 (over z, y_hi, core), fsdp: 8 (over y_lo, x).
Axes of the slice: x: 4, y: 4 (y_hi: 2, y_lo: 2; y = y_hi * 2 + y_lo), z: 8, core: 2. Of those that a mesh axis runs over, the one named last changes fastest.
Arguments:
- hidden: bfloat16 [131072, 1152], P(('dp', 'fsdp')), may hold values from -6 to 6
- text_ids: int32 [8192, 16], P(('dp', 'fsdp')), may hold values from 0 to 31999, as said below
- ln_gain: float32 [1152], replicated, may hold values from 0.5 to 1.5
- ln_bias: float32 [1152], replicated, may hold values from -2 to 2
- fc1_weight: bfloat16 [1152, 4304], P(None, 'fsdp'), may hold values from -0.1875 to 0.1875
- fc1_bias: float32 [4304], replicated, may hold values from -3 to 3
- fc2_weight: bfloat16 [4304, 1152], P('fsdp'), may hold values from -0.09375 to 0.09375
- fc2_bias: float32 [1152], replicated, may hold values from -3 to 3
- final_gain: float32 [1152], replicated, may hold values from 0.5 to 1.5
- final_bias: float32 [1152], replicated, may hold values from -0.2 to 0.2
- head_weight: bfloat16 [1152, 1152], replicated, may hold values from -0.1875 to 0.1875
- head_bias: float32 [1152], replicated, may hold values from -0.3 to 0.3
- image_emb: bfloat16 [8192, 1152], P(('dp', 'fsdp')), may hold values from -6 to 6
- teacher_logits: bfloat16 [8192, 12, 256], P('dp', None, 'fsdp'), may hold values from -12 to 12
- logit_scale: float32 [1], replicated, may hold values from 4 to 16
- logit_bias: float32 [1], replicated, may hold values from -3 to 0
Outputs:
- image_grad: float32 [8192, 1152], P(('dp', 'fsdp'))
Inputs may be any that keep to these rules, and one draw needn't show every extreme that they name: `text_ids`: 0 marks padding after a text's end; every text has at least one token and the tokens of a text come first.
All inputs are finite; a program needn't handle non-finite values.
Results may differ from a plain program's by a relative error of at most 0.0018.
Values may be sent and summed in bfloat16 or wider, within the bound.
No kernel may reach another device: no remote copies, remote signals or barrier semaphores. Data moves between devices by JAX's collectives and lax.ppermute only.
A program may use at most 128 MiB of HBM per device.

v0:
```python
import jax
import jax.numpy as jnp
from jax import lax
from jax.sharding import PartitionSpec as P


def from_everyone(array, axis):
    copies = jnp.broadcast_to(array, (lax.axis_size(axis), *array.shape))
    return lax.all_to_all(copies, axis, split_axis=0, concat_axis=0, tiled=True)


def joined_along(parts, dim):
    parts = jnp.moveaxis(parts, 0, dim)
    dims = parts.shape
    return parts.reshape(*dims[:dim], dims[dim] * dims[dim + 1], *dims[dim + 2 :])


def gather_directly(array, axis, dim):
    parts = from_everyone(array, axis)
    return joined_along(parts, dim)


def from_behind(array, axis, by):
    count = lax.axis_size(axis)
    return lax.ppermute(array, axis, [(i, (i + by) % count) for i in range(count)])


def layer_norm(values, gain, shift):
    centre = jnp.mean(values, axis=-1, keepdims=True)
    spread = jnp.mean((values - centre) ** 2, axis=-1, keepdims=True)
    return (values - centre) * lax.rsqrt(spread + 1e-06) * gain + shift


def on_device(
    hidden,
    text_ids,
    ln_gain,
    ln_bias,
    fc1_weight,
    fc1_bias,
    fc2_weight,
    fc2_bias,
    final_gain,
    final_bias,
    head_weight,
    head_bias,
    image_emb,
    teacher_logits,
    logit_scale,
    logit_bias,
):
    width = hidden.shape[1]
    texts_here, seq_len = text_ids.shape
    window = teacher_logits.shape[1]
    flat = hidden.astype(jnp.float32)
    normed = layer_norm(flat, ln_gain, ln_bias).astype(jnp.bfloat16)
    pre = (
        jnp.dot(
            normed,
            lax.all_gather(fc1_weight, "fsdp", axis=1, tiled=True),
            preferred_element_type=jnp.float32,
        )
        + fc1_bias
    )
    act = jax.nn.gelu(pre, approximate=True).astype(jnp.bfloat16)
    mixed = jnp.dot(
        act,
        lax.all_gather(fc2_weight, "fsdp", axis=0, tiled=True),
        preferred_element_type=jnp.float32,
    )
    out = flat + mixed + fc2_bias
    final = layer_norm(out, final_gain, final_bias).reshape(texts_here, seq_len, width)
    keep = (text_ids != 0).astype(jnp.float32)
    pooled = jnp.sum(final * keep[:, :, None], axis=1) / jnp.sum(keep, axis=1)[:, None]
    emb = (
        jnp.dot(pooled.astype(jnp.bfloat16), head_weight, preferred_element_type=jnp.float32)
        + head_bias
    )
    text_unit = (emb * lax.rsqrt(jnp.sum(emb * emb, axis=-1, keepdims=True) + 1e-06)).astype(
        jnp.bfloat16
    )
    group_units = gather_directly(text_unit, "fsdp", 0)
    images = image_emb.astype(jnp.float32)
    image_unit = (
        images * lax.rsqrt(jnp.sum(images * images, axis=-1, keepdims=True) + 1e-06)
    ).astype(jnp.bfloat16)
    scale = logit_scale[0]
    offset = logit_bias[0]

    def pair_term(units, pictures, tile):
        score = (
            scale
            * lax.dot_general(
                units, pictures, (((1,), (1,)), ((), ())), preferred_element_type=jnp.float32
            )
            + offset
        )
        weight = (jax.nn.sigmoid(score) - jax.nn.sigmoid(tile.astype(jnp.float32))).astype(
            jnp.bfloat16
        )
        return lax.dot_general(
            weight, units, (((0,), (0,)), ((), ())), preferred_element_type=jnp.float32
        )

    start_grad = jnp.zeros(image_unit.shape, jnp.float32)

    def turn_images(step, carry):
        pictures, total = carry
        tile = lax.dynamic_index_in_dim(teacher_logits, step, 1, keepdims=False)
        total = total + pair_term(group_units, pictures, tile)
        pictures, total = (
            from_behind(pictures.astype(jnp.float32), "dp", -1).astype(pictures.dtype),
            from_behind(total, "dp", -1),
        )
        return (pictures, total)

    pictures, total = lax.fori_loop(0, window - 1, turn_images, (image_unit, start_grad))
    total = total + pair_term(group_units, pictures, teacher_logits[:, window - 1, :])
    total = from_behind(total, "dp", window - 1)
    return scale * total


def solution(mesh):
    placed = (
        P(("dp", "fsdp"), None),
        P(("dp", "fsdp"), None),
        P(),
        P(),
        P(None, "fsdp"),
        P(),
        P("fsdp", None),
        P(),
        P(),
        P(),
        P(),
        P(),
        P(("dp", "fsdp"), None),
        P("dp", None, "fsdp"),
        P(),
        P(),
    )
    return jax.shard_map(
        on_device, mesh=mesh, in_specs=placed, out_specs=P(("dp", "fsdp"), None), check_vma=False
    )
```

profile of v0, /device:TPU:1, one launch (start us, length us, event | category | flops | bytes accessed | tf_op | source)
XLA Modules:
  0.0 442.1 jit_solution(9942454543745646307)
XLA Ops:
  11.5 111.0 %all-gather.5.cloned.1.call-done = bf16[8,538,1152]{2,1,0:T(8,128)(2,1)} async-done(((bf16[1,538,1152]{2,1,0:T(8,128)(2,1)}), bf16[8,538,1152]{2,1,0:T(8,128)(2,1)}) %all-gather.5.cloned.1.call-update) | async-done | bytes 9916432 | tf_op jit(solution)/shard_map/all_gather | solution.py:60
  122.5 11.8 %reshape.68 = bf16[4304,1152]{1,0:T(8,128)(2,1)} reshape(bf16[8,538,1152]{2,1,0:T(8,128)(2,1)} %all-gather.5.cloned.1.call-done) | data formatting | bytes 19832832
  134.4 98.5 %all-gather.7.cloned.1.call-done = bf16[8,538,1152]{2,1,0:T(8,128)(2,1)} async-done(((bf16[1,538,1152]{2,1,0:T(8,128)(2,1)}), bf16[8,538,1152]{2,1,0:T(8,128)(2,1)}) %all-gather.7.cloned.1.call-update) | async-done | bytes 9916432 | tf_op jit(solution)/shard_map/all_gather | solution.py:68
  232.9 11.9 %reshape.70 = bf16[4304,1152]{1,0:T(8,128)(2,1)} reshape(bf16[8,538,1152]{2,1,0:T(8,128)(2,1)} %all-gather.7.cloned.1.call-done) | data formatting | bytes 19832832
  244.8 23.1 %fusion.72 = (f32[512]{0:T(512)S(1)}, f32[512,1152]{1,0:T(8,128)}) fusion(f32[1152]{0:T(1024)S(1)} %copy-done.8, bf16[4304,1152]{1,0:T(8,128)(2,1)} %reshape.70, bf16[4304,1152]{1,0:T(8,128)(2,1)} %reshape.68, f32[4304]{0:T(1024)S(1)} %copy-done.7, bf16[512,1152]{1,0:T(8,128)(2,1)} %param.18, f32[1152]{0:T(1024)S(1)} %copy-done.9, f32[1152]{0:T(1024)S(1)} %copy-done.10, ...), kind=kOutput, calls=%fused_computation.91 | convolution fusion | flops 10182344704 | bytes 23408960 | tf_op jit(solution)/shard_map/dot_general | solution.py:66
  272.9 3.5 all-to-all-start
  277.8 9.5 %all-to-all-done = bf16[8,32,1152]{2,1,0:T(8,128)(2,1)S(1)} async-done(((bf16[8,32,1152]{2,1,0:T(8,128)(2,1)}), bf16[8,32,1152]{2,1,0:T(8,128)(2,1)S(1)}, u32[]{:S(2)}, u32[]{:S(2)}) %all-to-all-start) | async-done | bytes 589856 | tf_op jit(solution)/shard_map/all_to_all | solution.py:9
  287.3 134.7 %while.15 = (s32[]{:T(128)}, bf16[32,1152]{1,0:T(8,128)(2,1)S(1)}, f32[32,1152]{1,0:T(8,128)S(1)}, f32[]{:T(128)}, bf16[256,1152]{1,0:T(8,128)(2,1)S(1)}, /*inde...) while((s32[]{:T(128)}, bf16[32,1152]{1,0:T(8,128)(2,1)S(1)}, f32[32,1152]{1,0:T(8,128)S(1)}, f32[]{:T(128)}, ...), condition=%wide.region_9.10_spmd, body=%wide.region_8.9_spmd.sunk | while | flops 37875712 | bytes 2598565 | solution.py:117
  287.4 3.3 convolution_add_fusion.4
  291.4 4.8 %collective-permute-start = (bf16[32,1152]{1,0:T(8,128)(2,1)S(1)}, bf16[32,1152]{1,0:T(8,128)(2,1)S(1)}, u32[]{:S(2)}, u32[]{:S(2)}) collective-permute-start(bf16[32,1152]{1,0:T(8,128)(2,1)S(1)} %copy.24), channel_id=1, source_target_pairs={{0,248},{8,0},{16,8},{24,16},{32,24},{40,32},{48,40},{56,48},{64,5... | collective-permute-start | bytes 221192 | tf_op jit(solution)/shard_map/while/body/eval_jaxpr/ppermute | solution.py:25
  297.7 3.3 convolution_add_fusion.4
  303.2 5.5 %collective-permute-start = (bf16[32,1152]{1,0:T(8,128)(2,1)S(1)}, bf16[32,1152]{1,0:T(8,128)(2,1)S(1)}, u32[]{:S(2)}, u32[]{:S(2)}) collective-permute-start(bf16[32,1152]{1,0:T(8,128)(2,1)S(1)} %copy.24), channel_id=1, source_target_pairs={{0,248},{8,0},{16,8},{24,16},{32,24},{40,32},{48,40},{56,48},{64,5... | collective-permute-start | bytes 221192 | tf_op jit(solution)/shard_map/while/body/eval_jaxpr/ppermute | solution.py:25
  309.7 3.3 convolution_add_fusion.4
  312.9 2.7 collective-permute-start.1
  315.7 5.5 %collective-permute-start = (bf16[32,1152]{1,0:T(8,128)(2,1)S(1)}, bf16[32,1152]{1,0:T(8,128)(2,1)S(1)}, u32[]{:S(2)}, u32[]{:S(2)}) collective-permute-start(bf16[32,1152]{1,0:T(8,128)(2,1)S(1)} %copy.24), channel_id=1, source_target_pairs={{0,248},{8,0},{16,8},{24,16},{32,24},{40,32},{48,40},{56,48},{64,5... | collective-permute-start | bytes 221192 | tf_op jit(solution)/shard_map/while/body/eval_jaxpr/ppermute | solution.py:25
  322.1 3.3 convolution_add_fusion.4
  328.2 5.5 %collective-permute-start = (bf16[32,1152]{1,0:T(8,128)(2,1)S(1)}, bf16[32,1152]{1,0:T(8,128)(2,1)S(1)}, u32[]{:S(2)}, u32[]{:S(2)}) collective-permute-start(bf16[32,1152]{1,0:T(8,128)(2,1)S(1)} %copy.24), channel_id=1, source_target_pairs={{0,248},{8,0},{16,8},{24,16},{32,24},{40,32},{48,40},{56,48},{64,5... | collective-permute-start | bytes 221192 | tf_op jit(solution)/shard_map/while/body/eval_jaxpr/ppermute | solution.py:25
  334.6 3.3 convolution_add_fusion.4
  340.7 5.5 %collective-permute-start = (bf16[32,1152]{1,0:T(8,128)(2,1)S(1)}, bf16[32,1152]{1,0:T(8,128)(2,1)S(1)}, u32[]{:S(2)}, u32[]{:S(2)}) collective-permute-start(bf16[32,1152]{1,0:T(8,128)(2,1)S(1)} %copy.24), channel_id=1, source_target_pairs={{0,248},{8,0},{16,8},{24,16},{32,24},{40,32},{48,40},{56,48},{64,5... | collective-permute-start | bytes 221192 | tf_op jit(solution)/shard_map/while/body/eval_jaxpr/ppermute | solution.py:25
  347.1 3.3 convolution_add_fusion.4
  353.1 5.5 %collective-permute-start = (bf16[32,1152]{1,0:T(8,128)(2,1)S(1)}, bf16[32,1152]{1,0:T(8,128)(2,1)S(1)}, u32[]{:S(2)}, u32[]{:S(2)}) collective-permute-start(bf16[32,1152]{1,0:T(8,128)(2,1)S(1)} %copy.24), channel_id=1, source_target_pairs={{0,248},{8,0},{16,8},{24,16},{32,24},{40,32},{48,40},{56,48},{64,5... | collective-permute-start | bytes 221192 | tf_op jit(solution)/shard_map/while/body/eval_jaxpr/ppermute | solution.py:25
  359.6 3.3 convolution_add_fusion.4
  365.6 5.5 %collective-permute-start = (bf16[32,1152]{1,0:T(8,128)(2,1)S(1)}, bf16[32,1152]{1,0:T(8,128)(2,1)S(1)}, u32[]{:S(2)}, u32[]{:S(2)}) collective-permute-start(bf16[32,1152]{1,0:T(8,128)(2,1)S(1)} %copy.24), channel_id=1, source_target_pairs={{0,248},{8,0},{16,8},{24,16},{32,24},{40,32},{48,40},{56,48},{64,5... | collective-permute-start | bytes 221192 | tf_op jit(solution)/shard_map/while/body/eval_jaxpr/ppermute | solution.py:25
  372.1 3.3 convolution_add_fusion.4
  378.1 5.5 %collective-permute-start = (bf16[32,1152]{1,0:T(8,128)(2,1)S(1)}, bf16[32,1152]{1,0:T(8,128)(2,1)S(1)}, u32[]{:S(2)}, u32[]{:S(2)}) collective-permute-start(bf16[32,1152]{1,0:T(8,128)(2,1)S(1)} %copy.24), channel_id=1, source_target_pairs={{0,248},{8,0},{16,8},{24,16},{32,24},{40,32},{48,40},{56,48},{64,5... | collective-permute-start | bytes 221192 | tf_op jit(solution)/shard_map/while/body/eval_jaxpr/ppermute | solution.py:25
  384.6 3.3 convolution_add_fusion.4
  390.6 5.5 %collective-permute-start = (bf16[32,1152]{1,0:T(8,128)(2,1)S(1)}, bf16[32,1152]{1,0:T(8,128)(2,1)S(1)}, u32[]{:S(2)}, u32[]{:S(2)}) collective-permute-start(bf16[32,1152]{1,0:T(8,128)(2,1)S(1)} %copy.24), channel_id=1, source_target_pairs={{0,248},{8,0},{16,8},{24,16},{32,24},{40,32},{48,40},{56,48},{64,5... | collective-permute-start | bytes 221192 | tf_op jit(solution)/shard_map/while/body/eval_jaxpr/ppermute | solution.py:25
  397.1 3.3 convolution_add_fusion.4
  403.1 5.5 %collective-permute-start = (bf16[32,1152]{1,0:T(8,128)(2,1)S(1)}, bf16[32,1152]{1,0:T(8,128)(2,1)S(1)}, u32[]{:S(2)}, u32[]{:S(2)}) collective-permute-start(bf16[32,1152]{1,0:T(8,128)(2,1)S(1)} %copy.24), channel_id=1, source_target_pairs={{0,248},{8,0},{16,8},{24,16},{32,24},{40,32},{48,40},{56,48},{64,5... | collective-permute-start | bytes 221192 | tf_op jit(solution)/shard_map/while/body/eval_jaxpr/ppermute | solution.py:25
  409.5 3.3 convolution_add_fusion.4
  415.6 5.5 %collective-permute-start = (bf16[32,1152]{1,0:T(8,128)(2,1)S(1)}, bf16[32,1152]{1,0:T(8,128)(2,1)S(1)}, u32[]{:S(2)}, u32[]{:S(2)}) collective-permute-start(bf16[32,1152]{1,0:T(8,128)(2,1)S(1)} %copy.24), channel_id=1, source_target_pairs={{0,248},{8,0},{16,8},{24,16},{32,24},{40,32},{48,40},{56,48},{64,5... | collective-permute-start | bytes 221192 | tf_op jit(solution)/shard_map/while/body/eval_jaxpr/ppermute | solution.py:25
  424.0 10.6 %collective-permute-done.2 = f32[32,1152]{1,0:T(8,128)S(1)} collective-permute-done((f32[32,1152]{1,0:T(8,128)}, f32[32,1152]{1,0:T(8,128)S(1)}, u32[]{:S(2)}, u32[]{:S(2)}) %collective-permute-start.2) | collective-permute-done | bytes 147488 | tf_op jit(solution)/shard_map/ppermute | solution.py:25
  (91 shorter events, 48.2 us)
Async XLA Ops:
  6.5 264.6 %copy-start = (bf16[1152,1152]{1,0:T(8,128)(2,1)S(1)}, bf16[1152,1152]{1,0:T(8,128)(2,1)}, u32[]{:S(2)}) copy-start(bf16[1152,1152]{1,0:T(8,128)(2,1)} %param.28) | copy-start | bytes 7962628
  6.5 116.0 %all-gather.5.cloned.1.call-start = ((), (), s32[]{:S(2)}) async-start(), calls=%async_computation.1 | async-start | bytes 11280384 | tf_op jit(solution)/shard_map/all_gather | solution.py:60
  7.3 225.6 %all-gather.7.cloned.1.call-start = ((), (), s32[]{:S(2)}) async-start(), calls=%async_computation.2 | async-start | bytes 11280384 | tf_op jit(solution)/shard_map/all_gather | solution.py:68
  134.3 110.5 %copy-start.7 = (f32[4304]{0:T(1024)S(1)}, f32[4304]{0:T(1024)}, u32[]{:S(2)}) copy-start(f32[4304]{0:T(1024)} %param.23) | copy-start | bytes 51652
  134.4 110.5 %copy-start.8 = (f32[1152]{0:T(1024)S(1)}, f32[1152]{0:T(1024)}, u32[]{:S(2)}) copy-start(f32[1152]{0:T(1024)} %param.25) | copy-start | bytes 13828
  134.4 110.5 %copy-start.9 = (f32[1152]{0:T(1024)S(1)}, f32[1152]{0:T(1024)}, u32[]{:S(2)}) copy-start(f32[1152]{0:T(1024)} %param.21) | copy-start | bytes 13828
  134.4 110.5 %copy-start.10 = (f32[1152]{0:T(1024)S(1)}, f32[1152]{0:T(1024)}, u32[]{:S(2)}) copy-start(f32[1152]{0:T(1024)} %param.20) | copy-start | bytes 13828
  244.8 25.3 %copy-start.5 = (f32[1152]{0:T(1024)S(1)}, f32[1152]{0:T(1024)}, u32[]{:S(2)}) copy-start(f32[1152]{0:T(1024)} %param.26) | copy-start | bytes 13828
  272.9 14.4 %all-to-all-start = ((bf16[8,32,1152]{2,1,0:T(8,128)(2,1)}), bf16[8,32,1152]{2,1,0:T(8,128)(2,1)S(1)}, u32[]{:S(2)}, u32[]{:S(2)}) async-start(bf16[8,32,1152]{2,1,0:T(8,128)(2,1)} %broadcast_in_dim.5), calls=%async_computation | async-start | bytes 1179648 | tf_op jit(solution)/shard_map/all_to_all | solution.py:9
  290.7 7.1 %collective-permute-start.1 = (f32[32,1152]{1,0:T(8,128)}, f32[32,1152]{1,0:T(8,128)S(1)}, u32[]{:S(2)}, u32[]{:S(2)}) collective-permute-start(f32[32,1152]{1,0:T(8,128)} %convolution_add_fusion.4), channel_id=1, source_target_pairs={{0,248},{8,0},{16,8},{24,16},{32,24},{40,32},{48,40},{56,48},{64,5... | collective-permute-start | bytes 442376 | tf_op jit(solution)/shard_map/while/body/eval_jaxpr/ppermute | solution.py:25
  291.4 6.3 %collective-permute-start = (bf16[32,1152]{1,0:T(8,128)(2,1)S(1)}, bf16[32,1152]{1,0:T(8,128)(2,1)S(1)}, u32[]{:S(2)}, u32[]{:S(2)}) collective-permute-start(bf16[32,1152]{1,0:T(8,128)(2,1)S(1)} %copy.24), channel_id=1, source_target_pairs={{0,248},{8,0},{16,8},{24,16},{32,24},{40,32},{48,40},{56,48},{64,5... | collective-permute-start | bytes 221192 | tf_op jit(solution)/shard_map/while/body/eval_jaxpr/ppermute | solution.py:25
  301.0 8.6 %collective-permute-start.1 = (f32[32,1152]{1,0:T(8,128)}, f32[32,1152]{1,0:T(8,128)S(1)}, u32[]{:S(2)}, u32[]{:S(2)}) collective-permute-start(f32[32,1152]{1,0:T(8,128)} %convolution_add_fusion.4), channel_id=1, source_target_pairs={{0,248},{8,0},{16,8},{24,16},{32,24},{40,32},{48,40},{56,48},{64,5... | collective-permute-start | bytes 442376 | tf_op jit(solution)/shard_map/while/body/eval_jaxpr/ppermute | solution.py:25
  303.2 6.4 %collective-permute-start = (bf16[32,1152]{1,0:T(8,128)(2,1)S(1)}, bf16[32,1152]{1,0:T(8,128)(2,1)S(1)}, u32[]{:S(2)}, u32[]{:S(2)}) collective-permute-start(bf16[32,1152]{1,0:T(8,128)(2,1)S(1)} %copy.24), channel_id=1, source_target_pairs={{0,248},{8,0},{16,8},{24,16},{32,24},{40,32},{48,40},{56,48},{64,5... | collective-permute-start | bytes 221192 | tf_op jit(solution)/shard_map/while/body/eval_jaxpr/ppermute | solution.py:25
  312.9 9.2 %collective-permute-start.1 = (f32[32,1152]{1,0:T(8,128)}, f32[32,1152]{1,0:T(8,128)S(1)}, u32[]{:S(2)}, u32[]{:S(2)}) collective-permute-start(f32[32,1152]{1,0:T(8,128)} %convolution_add_fusion.4), channel_id=1, source_target_pairs={{0,248},{8,0},{16,8},{24,16},{32,24},{40,32},{48,40},{56,48},{64,5... | collective-permute-start | bytes 442376 | tf_op jit(solution)/shard_map/while/body/eval_jaxpr/ppermute | solution.py:25
  315.7 6.4 %collective-permute-start = (bf16[32,1152]{1,0:T(8,128)(2,1)S(1)}, bf16[32,1152]{1,0:T(8,128)(2,1)S(1)}, u32[]{:S(2)}, u32[]{:S(2)}) collective-permute-start(bf16[32,1152]{1,0:T(8,128)(2,1)S(1)} %copy.24), channel_id=1, source_target_pairs={{0,248},{8,0},{16,8},{24,16},{32,24},{40,32},{48,40},{56,48},{64,5... | collective-permute-start | bytes 221192 | tf_op jit(solution)/shard_map/while/body/eval_jaxpr/ppermute | solution.py:25
  325.4 9.2 %collective-permute-start.1 = (f32[32,1152]{1,0:T(8,128)}, f32[32,1152]{1,0:T(8,128)S(1)}, u32[]{:S(2)}, u32[]{:S(2)}) collective-permute-start(f32[32,1152]{1,0:T(8,128)} %convolution_add_fusion.4), channel_id=1, source_target_pairs={{0,248},{8,0},{16,8},{24,16},{32,24},{40,32},{48,40},{56,48},{64,5... | collective-permute-start | bytes 442376 | tf_op jit(solution)/shard_map/while/body/eval_jaxpr/ppermute | solution.py:25
  328.2 6.4 %collective-permute-start = (bf16[32,1152]{1,0:T(8,128)(2,1)S(1)}, bf16[32,1152]{1,0:T(8,128)(2,1)S(1)}, u32[]{:S(2)}, u32[]{:S(2)}) collective-permute-start(bf16[32,1152]{1,0:T(8,128)(2,1)S(1)} %copy.24), channel_id=1, source_target_pairs={{0,248},{8,0},{16,8},{24,16},{32,24},{40,32},{48,40},{56,48},{64,5... | collective-permute-start | bytes 221192 | tf_op jit(solution)/shard_map/while/body/eval_jaxpr/ppermute | solution.py:25
  337.9 9.2 %collective-permute-start.1 = (f32[32,1152]{1,0:T(8,128)}, f32[32,1152]{1,0:T(8,128)S(1)}, u32[]{:S(2)}, u32[]{:S(2)}) collective-permute-start(f32[32,1152]{1,0:T(8,128)} %convolution_add_fusion.4), channel_id=1, source_target_pairs={{0,248},{8,0},{16,8},{24,16},{32,24},{40,32},{48,40},{56,48},{64,5... | collective-permute-start | bytes 442376 | tf_op jit(solution)/shard_map/while/body/eval_jaxpr/ppermute | solution.py:25
  340.7 6.4 %collective-permute-start = (bf16[32,1152]{1,0:T(8,128)(2,1)S(1)}, bf16[32,1152]{1,0:T(8,128)(2,1)S(1)}, u32[]{:S(2)}, u32[]{:S(2)}) collective-permute-start(bf16[32,1152]{1,0:T(8,128)(2,1)S(1)} %copy.24), channel_id=1, source_target_pairs={{0,248},{8,0},{16,8},{24,16},{32,24},{40,32},{48,40},{56,48},{64,5... | collective-permute-start | bytes 221192 | tf_op jit(solution)/shard_map/while/body/eval_jaxpr/ppermute | solution.py:25
  350.4 9.2 %collective-permute-start.1 = (f32[32,1152]{1,0:T(8,128)}, f32[32,1152]{1,0:T(8,128)S(1)}, u32[]{:S(2)}, u32[]{:S(2)}) collective-permute-start(f32[32,1152]{1,0:T(8,128)} %convolution_add_fusion.4), channel_id=1, source_target_pairs={{0,248},{8,0},{16,8},{24,16},{32,24},{40,32},{48,40},{56,48},{64,5... | collective-permute-start | bytes 442376 | tf_op jit(solution)/shard_map/while/body/eval_jaxpr/ppermute | solution.py:25
  353.1 6.4 %collective-permute-start = (bf16[32,1152]{1,0:T(8,128)(2,1)S(1)}, bf16[32,1152]{1,0:T(8,128)(2,1)S(1)}, u32[]{:S(2)}, u32[]{:S(2)}) collective-permute-start(bf16[32,1152]{1,0:T(8,128)(2,1)S(1)} %copy.24), channel_id=1, source_target_pairs={{0,248},{8,0},{16,8},{24,16},{32,24},{40,32},{48,40},{56,48},{64,5... | collective-permute-start | bytes 221192 | tf_op jit(solution)/shard_map/while/body/eval_jaxpr/ppermute | solution.py:25
  362.9 9.2 %collective-permute-start.1 = (f32[32,1152]{1,0:T(8,128)}, f32[32,1152]{1,0:T(8,128)S(1)}, u32[]{:S(2)}, u32[]{:S(2)}) collective-permute-start(f32[32,1152]{1,0:T(8,128)} %convolution_add_fusion.4), channel_id=1, source_target_pairs={{0,248},{8,0},{16,8},{24,16},{32,24},{40,32},{48,40},{56,48},{64,5... | collective-permute-start | bytes 442376 | tf_op jit(solution)/shard_map/while/body/eval_jaxpr/ppermute | solution.py:25
  365.6 6.4 %collective-permute-start = (bf16[32,1152]{1,0:T(8,128)(2,1)S(1)}, bf16[32,1152]{1,0:T(8,128)(2,1)S(1)}, u32[]{:S(2)}, u32[]{:S(2)}) collective-permute-start(bf16[32,1152]{1,0:T(8,128)(2,1)S(1)} %copy.24), channel_id=1, source_target_pairs={{0,248},{8,0},{16,8},{24,16},{32,24},{40,32},{48,40},{56,48},{64,5... | collective-permute-start | bytes 221192 | tf_op jit(solution)/shard_map/while/body/eval_jaxpr/ppermute | solution.py:25
  375.4 9.2 %collective-permute-start.1 = (f32[32,1152]{1,0:T(8,128)}, f32[32,1152]{1,0:T(8,128)S(1)}, u32[]{:S(2)}, u32[]{:S(2)}) collective-permute-start(f32[32,1152]{1,0:T(8,128)} %convolution_add_fusion.4), channel_id=1, source_target_pairs={{0,248},{8,0},{16,8},{24,16},{32,24},{40,32},{48,40},{56,48},{64,5... | collective-permute-start | bytes 442376 | tf_op jit(solution)/shard_map/while/body/eval_jaxpr/ppermute | solution.py:25
  378.1 6.4 %collective-permute-start = (bf16[32,1152]{1,0:T(8,128)(2,1)S(1)}, bf16[32,1152]{1,0:T(8,128)(2,1)S(1)}, u32[]{:S(2)}, u32[]{:S(2)}) collective-permute-start(bf16[32,1152]{1,0:T(8,128)(2,1)S(1)} %copy.24), channel_id=1, source_target_pairs={{0,248},{8,0},{16,8},{24,16},{32,24},{40,32},{48,40},{56,48},{64,5... | collective-permute-start | bytes 221192 | tf_op jit(solution)/shard_map/while/body/eval_jaxpr/ppermute | solution.py:25
  387.9 9.2 %collective-permute-start.1 = (f32[32,1152]{1,0:T(8,128)}, f32[32,1152]{1,0:T(8,128)S(1)}, u32[]{:S(2)}, u32[]{:S(2)}) collective-permute-start(f32[32,1152]{1,0:T(8,128)} %convolution_add_fusion.4), channel_id=1, source_target_pairs={{0,248},{8,0},{16,8},{24,16},{32,24},{40,32},{48,40},{56,48},{64,5... | collective-permute-start | bytes 442376 | tf_op jit(solution)/shard_map/while/body/eval_jaxpr/ppermute | solution.py:25
  390.6 6.4 %collective-permute-start = (bf16[32,1152]{1,0:T(8,128)(2,1)S(1)}, bf16[32,1152]{1,0:T(8,128)(2,1)S(1)}, u32[]{:S(2)}, u32[]{:S(2)}) collective-permute-start(bf16[32,1152]{1,0:T(8,128)(2,1)S(1)} %copy.24), channel_id=1, source_target_pairs={{0,248},{8,0},{16,8},{24,16},{32,24},{40,32},{48,40},{56,48},{64,5... | collective-permute-start | bytes 221192 | tf_op jit(solution)/shard_map/while/body/eval_jaxpr/ppermute | solution.py:25
  400.3 9.2 %collective-permute-start.1 = (f32[32,1152]{1,0:T(8,128)}, f32[32,1152]{1,0:T(8,128)S(1)}, u32[]{:S(2)}, u32[]{:S(2)}) collective-permute-start(f32[32,1152]{1,0:T(8,128)} %convolution_add_fusion.4), channel_id=1, source_target_pairs={{0,248},{8,0},{16,8},{24,16},{32,24},{40,32},{48,40},{56,48},{64,5... | collective-permute-start | bytes 442376 | tf_op jit(solution)/shard_map/while/body/eval_jaxpr/ppermute | solution.py:25
  403.1 6.4 %collective-permute-start = (bf16[32,1152]{1,0:T(8,128)(2,1)S(1)}, bf16[32,1152]{1,0:T(8,128)(2,1)S(1)}, u32[]{:S(2)}, u32[]{:S(2)}) collective-permute-start(bf16[32,1152]{1,0:T(8,128)(2,1)S(1)} %copy.24), channel_id=1, source_target_pairs={{0,248},{8,0},{16,8},{24,16},{32,24},{40,32},{48,40},{56,48},{64,5... | collective-permute-start | bytes 221192 | tf_op jit(solution)/shard_map/while/body/eval_jaxpr/ppermute | solution.py:25
  412.8 9.2 %collective-permute-start.1 = (f32[32,1152]{1,0:T(8,128)}, f32[32,1152]{1,0:T(8,128)S(1)}, u32[]{:S(2)}, u32[]{:S(2)}) collective-permute-start(f32[32,1152]{1,0:T(8,128)} %convolution_add_fusion.4), channel_id=1, source_target_pairs={{0,248},{8,0},{16,8},{24,16},{32,24},{40,32},{48,40},{56,48},{64,5... | collective-permute-start | bytes 442376 | tf_op jit(solution)/shard_map/while/body/eval_jaxpr/ppermute | solution.py:25
  415.6 6.4 %collective-permute-start = (bf16[32,1152]{1,0:T(8,128)(2,1)S(1)}, bf16[32,1152]{1,0:T(8,128)(2,1)S(1)}, u32[]{:S(2)}, u32[]{:S(2)}) collective-permute-start(bf16[32,1152]{1,0:T(8,128)(2,1)S(1)} %copy.24), channel_id=1, source_target_pairs={{0,248},{8,0},{16,8},{24,16},{32,24},{40,32},{48,40},{56,48},{64,5... | collective-permute-start | bytes 221192 | tf_op jit(solution)/shard_map/while/body/eval_jaxpr/ppermute | solution.py:25
  424.0 10.6 %collective-permute-start.2 = (f32[32,1152]{1,0:T(8,128)}, f32[32,1152]{1,0:T(8,128)S(1)}, u32[]{:S(2)}, u32[]{:S(2)}) collective-permute-start(f32[32,1152]{1,0:T(8,128)} %convolution_add_fusion.1), channel_id=1, source_target_pairs={{0,88},{8,96},{16,104},{24,112},{32,120},{40,128},{48,136},{56,144... | collective-permute-start | bytes 442376 | tf_op jit(solution)/shard_map/ppermute | solution.py:25
  (5 other events, 11.1 us)
Sparse Core Ops, SparseCore 0:
  9.1 113.3 all-gather.4
  124.3 108.5 all-gather.6
where the time goes:
time: 444 us; the launch traced here: 442 us
  waiting for transfers between devices  242 us (55%)
  starting transfers between devices  91.3 us (21%)
  matrix products  62 us (14%)
  local copies, waits for them, and re-layouts  25 us (6%)
  between operations  14.8 us (3%)
  other arithmetic  7.29 us (2%)
    all_gather x1, waiting for transfers between devices, on_device(): lax.all_gather(fc1_weight, 'fsdp', axis=1, tiled=True)  111 us
    all_gather x1, waiting for transfers between devices, on_device(): lax.all_gather(fc2_weight, 'fsdp', axis=0, tiled=True)  98.5 us
    ppermute x23, starting transfers between devices, from_behind(): lax.ppermute(array, axis, [(i, (i + by) % count) for i in range(count)])  87.7 us
    dot_general x12, matrix products, pair_term(): lax.dot_general(weight, units, (((0,), (0,)), ((), ())), preferred_elemen...  38.2 us
    unnamed x24, local copies, waits for them, and re-layouts  23.9 us
    dot_general x1, matrix products, on_device(): jnp.dot(act, lax.all_gather(fc2_weight, 'fsdp', axis=0, tiled=True), pref...  23.1 us
    ppermute x23, waiting for transfers between devices, from_behind(): lax.ppermute(array, axis, [(i, (i + by) % count) for i in range(count)])  21.2 us
    all_to_all x1, waiting for transfers between devices, from_everyone(): return lax.all_to_all(copies, axis, split_axis=0, concat_axis=0, tiled=True)  9.5 us
  transfers between devices with their start and end apart: 26, of which 15 were waited for; matrix products, arithmetic and copies ran while one was open for 3% of the time, Pallas kernels for 0%

commit v1 on v0

--- a/solution.py
+++ b/solution.py
@@ -65,7 +65,9 @@
     act = jax.nn.gelu(pre, approximate=True).astype(jnp.bfloat16)
     mixed = jnp.dot(
         act,
-        lax.all_gather(fc2_weight, "fsdp", axis=0, tiled=True),
+        jnp.concatenate(
+            lax.all_to_all(jnp.stack([fc2_weight] * lax.axis_size("fsdp")), "fsdp", 0, 0), axis=0
+        ),
         preferred_element_type=jnp.float32,
     )
     out = flat + mixed + fc2_bias

time: 444 us -> 481 us (1.083)
  waiting for transfers between devices: 242 us -> 259 us
  starting transfers between devices: 91.3 us -> 105 us
  local copies, waits for them, and re-layouts: 25 us -> 30.8 us
    all_to_all x0 -> x1, waiting for transfers between devices: none -> 170 us  [on_device(): lax.all_to_all(jnp.stack([fc2_weight] * lax.axis_size('fsdp')), 'fsdp', 0...]
    all_gather x1 -> x0, waiting for transfers between devices: 98.5 us -> none  [on_device(): lax.all_gather(fc2_weight, 'fsdp', axis=0, tiled=True)]
    all_gather x1, waiting for transfers between devices: 111 us -> 58.2 us  [on_device(): lax.all_gather(fc1_weight, 'fsdp', axis=1, tiled=True)]
    unnamed x24 -> x23, local copies, waits for them, and re-layouts: 23.9 us -> 12.1 us
    reshape x0 -> x1, local copies, waits for them, and re-layouts: none -> 11.8 us  [on_device(): jnp.concatenate(lax.all_to_all(jnp.stack([fc2_weight] * lax.axis_size('fs...]
    all_to_all x0 -> x1, starting transfers between devices: none -> 5.98 us  [on_device(): lax.all_to_all(jnp.stack([fc2_weight] * lax.axis_size('fsdp')), 'fsdp', 0...]
    another operation x11 -> x12, local copies, waits for them, and re-layouts: 0.07 us -> 5.92 us  [the longest x1 5.85 us: on_device(): jnp.stack([fc2_weight] * lax.axis_size('fsdp'))]
    ppermute x23, starting transfers between devices: 87.7 us -> 93.1 us  [from_behind(): lax.ppermute(array, axis, [(i, (i + by) % count) for i in range(count)])]
  transfers between devices with their start and end apart: 26 -> 26, of which waited for: 15 -> 15; matrix products, arithmetic and copies ran while one was open for 3% -> 4% of each run, Pallas kernels for 0% -> 0%
where the time goes in v1:
time: 481 us; the launch traced here: 479 us
  waiting for transfers between devices  259 us (54%)
  starting transfers between devices  105 us (22%)
  matrix products  62 us (13%)
  local copies, waits for them, and re-layouts  30.8 us (6%)
  between operations  14.8 us (3%)
  other arithmetic  7.29 us (2%)
    all_to_all x1, waiting for transfers between devices, on_device(): lax.all_to_all(jnp.stack([fc2_weight] * lax.axis_size('fsdp')), 'fsdp', 0...  170 us
    ppermute x23, starting transfers between devices, from_behind(): lax.ppermute(array, axis, [(i, (i + by) % count) for i in range(count)])  93.1 us
    all_gather x1, waiting for transfers between devices, on_device(): lax.all_gather(fc1_weight, 'fsdp', axis=1, tiled=True)  58.2 us
    dot_general x12, matrix products, pair_term(): lax.dot_general(weight, units, (((0,), (0,)), ((), ())), preferred_elemen...  38.2 us
    dot_general x1, matrix products, on_device(): jnp.dot(act, jnp.concatenate(lax.all_to_all(jnp.stack([fc2_weight] * lax....  23.1 us
    ppermute x23, waiting for transfers between devices, from_behind(): lax.ppermute(array, axis, [(i, (i + by) % count) for i in range(count)])  20.4 us
    unnamed x23, local copies, waits for them, and re-layouts  12.1 us
    reshape x1, local copies, waits for them, and re-layouts, on_device(): jnp.concatenate(lax.all_to_all(jnp.stack([fc2_weight] * lax.axis_size('fs...  11.8 us
  transfers between devices with their start and end apart: 26, of which 15 were waited for; matrix products, arithmetic and copies ran while one was open for 4% of the time, Pallas kernels for 0%

profile of v1, /device:TPU:1, one launch (start us, length us, event | category | flops | bytes accessed | tf_op | source)
XLA Modules:
  0.0 479.0 jit_solution(11411972320996159858)
XLA Ops:
  7.3 5.8 %stack.2 = bf16[8,538,1152]{2,1,0:T(8,128)(2,1)} broadcast(bf16[538,1152]{1,0:T(8,128)(2,1)} %param.24), dimensions={1,2} | broadcast | bytes 11155968 | tf_op jit(solution)/shard_map/stack | solution.py:69
  13.1 6.0 %all-to-all-start = ((bf16[8,538,1152]{2,1,0:T(8,128)(2,1)}), bf16[8,538,1152]{2,1,0:T(8,128)(2,1)}, u32[]{:S(2)}, u32[]{:S(2)}) async-start(bf16[8,538,1152]{2,1,0:T(8,128)(2,1)} %stack.2), calls=%async_computation | async-start | bytes 20054016 | tf_op jit(solution)/shard_map/all_to_all | solution.py:69
  22.6 170.2 %all-to-all-done = bf16[8,538,1152]{2,1,0:T(8,128)(2,1)} async-done(((bf16[8,538,1152]{2,1,0:T(8,128)(2,1)}), bf16[8,538,1152]{2,1,0:T(8,128)(2,1)}, u32[]{:S(2)}, u32[]{:S(2)}) %all-to-all-start) | async-done | bytes 9916448 | tf_op jit(solution)/shard_map/all_to_all | solution.py:69
  192.7 11.8 %reshape.66 = bf16[4304,1152]{1,0:T(8,128)(2,1)} reshape(bf16[8,538,1152]{2,1,0:T(8,128)(2,1)} %all-to-all-done) | data formatting | bytes 19832832 | tf_op jit(solution)/shard_map/reshape | solution.py:68
  204.6 58.2 %all-gather.3.cloned.1.call-done = bf16[8,538,1152]{2,1,0:T(8,128)(2,1)} async-done(((bf16[1,538,1152]{2,1,0:T(8,128)(2,1)}), bf16[8,538,1152]{2,1,0:T(8,128)(2,1)}) %all-gather.3.cloned.1.call-update) | async-done | bytes 9916432 | tf_op jit(solution)/shard_map/all_gather | solution.py:60
  262.7 11.9 %reshape.74 = bf16[4304,1152]{1,0:T(8,128)(2,1)} reshape(bf16[8,538,1152]{2,1,0:T(8,128)(2,1)} %all-gather.3.cloned.1.call-done) | data formatting | bytes 19832832
  274.7 23.1 %fusion.72 = (f32[512]{0:T(512)S(1)}, f32[512,1152]{1,0:T(8,128)}) fusion(f32[1152]{0:T(1024)S(1)} %copy-done.8, bf16[4304,1152]{1,0:T(8,128)(2,1)} %reshape.66, bf16[4304,1152]{1,0:T(8,128)(2,1)} %reshape.74, f32[4304]{0:T(1024)S(1)} %copy-done.7, bf16[512,1152]{1,0:T(8,128)(2,1)} %param.18, f32[1152]{0:T(1024)S(1)} %copy-done.9, f32[1152]{0:T(1024)S(1)} %copy-done.10, ...), kind=kOutput, calls=%fused_computation.91 | convolution fusion | flops 10182344704 | bytes 23408960 | tf_op jit(solution)/shard_map/dot_general | solution.py:66
  302.7 5.9 %all-to-all-start.1 = ((bf16[8,32,1152]{2,1,0:T(8,128)(2,1)}), bf16[8,32,1152]{2,1,0:T(8,128)(2,1)S(1)}, u32[]{:S(2)}, u32[]{:S(2)}) async-start(bf16[8,32,1152]{2,1,0:T(8,128)(2,1)} %broadcast_in_dim.5), calls=%async_computation.1 | async-start | bytes 1179648 | tf_op jit(solution)/shard_map/all_to_all | solution.py:9
  310.1 9.6 %all-to-all-done.1 = bf16[8,32,1152]{2,1,0:T(8,128)(2,1)S(1)} async-done(((bf16[8,32,1152]{2,1,0:T(8,128)(2,1)}), bf16[8,32,1152]{2,1,0:T(8,128)(2,1)S(1)}, u32[]{:S(2)}, u32[]{:S(2)}) %all-to-all-start.1) | async-done | bytes 589856 | tf_op jit(solution)/shard_map/all_to_all | solution.py:9
  319.6 139.5 %while.15 = (s32[]{:T(128)}, bf16[32,1152]{1,0:T(8,128)(2,1)S(1)}, f32[32,1152]{1,0:T(8,128)S(1)}, f32[]{:T(128)}, bf16[256,1152]{1,0:T(8,128)(2,1)S(1)}, /*inde...) while((s32[]{:T(128)}, bf16[32,1152]{1,0:T(8,128)(2,1)S(1)}, f32[32,1152]{1,0:T(8,128)S(1)}, f32[]{:T(128)}, ...), condition=%wide.region_9.10_spmd, body=%wide.region_8.9_spmd.sunk | while | flops 37875712 | bytes 2598565 | solution.py:119
  319.7 3.3 convolution_add_fusion.4
  323.7 9.6 %collective-permute-start = (bf16[32,1152]{1,0:T(8,128)(2,1)S(1)}, bf16[32,1152]{1,0:T(8,128)(2,1)S(1)}, u32[]{:S(2)}, u32[]{:S(2)}) collective-permute-start(bf16[32,1152]{1,0:T(8,128)(2,1)S(1)} %copy.24), channel_id=1, source_target_pairs={{0,248},{8,0},{16,8},{24,16},{32,24},{40,32},{48,40},{56,48},{64,5... | collective-permute-start | bytes 221192 | tf_op jit(solution)/shard_map/while/body/eval_jaxpr/ppermute | solution.py:25
  334.3 3.3 convolution_add_fusion.4
  340.3 5.5 %collective-permute-start = (bf16[32,1152]{1,0:T(8,128)(2,1)S(1)}, bf16[32,1152]{1,0:T(8,128)(2,1)S(1)}, u32[]{:S(2)}, u32[]{:S(2)}) collective-permute-start(bf16[32,1152]{1,0:T(8,128)(2,1)S(1)} %copy.24), channel_id=1, source_target_pairs={{0,248},{8,0},{16,8},{24,16},{32,24},{40,32},{48,40},{56,48},{64,5... | collective-permute-start | bytes 221192 | tf_op jit(solution)/shard_map/while/body/eval_jaxpr/ppermute | solution.py:25
  346.8 3.3 convolution_add_fusion.4
  352.8 5.5 %collective-permute-start = (bf16[32,1152]{1,0:T(8,128)(2,1)S(1)}, bf16[32,1152]{1,0:T(8,128)(2,1)S(1)}, u32[]{:S(2)}, u32[]{:S(2)}) collective-permute-start(bf16[32,1152]{1,0:T(8,128)(2,1)S(1)} %copy.24), channel_id=1, source_target_pairs={{0,248},{8,0},{16,8},{24,16},{32,24},{40,32},{48,40},{56,48},{64,5... | collective-permute-start | bytes 221192 | tf_op jit(solution)/shard_map/while/body/eval_jaxpr/ppermute | solution.py:25
  359.3 3.3 convolution_add_fusion.4
  365.3 5.5 %collective-permute-start = (bf16[32,1152]{1,0:T(8,128)(2,1)S(1)}, bf16[32,1152]{1,0:T(8,128)(2,1)S(1)}, u32[]{:S(2)}, u32[]{:S(2)}) collective-permute-start(bf16[32,1152]{1,0:T(8,128)(2,1)S(1)} %copy.24), channel_id=1, source_target_pairs={{0,248},{8,0},{16,8},{24,16},{32,24},{40,32},{48,40},{56,48},{64,5... | collective-permute-start | bytes 221192 | tf_op jit(solution)/shard_map/while/body/eval_jaxpr/ppermute | solution.py:25
  371.8 3.3 convolution_add_fusion.4
  377.8 5.5 %collective-permute-start = (bf16[32,1152]{1,0:T(8,128)(2,1)S(1)}, bf16[32,1152]{1,0:T(8,128)(2,1)S(1)}, u32[]{:S(2)}, u32[]{:S(2)}) collective-permute-start(bf16[32,1152]{1,0:T(8,128)(2,1)S(1)} %copy.24), channel_id=1, source_target_pairs={{0,248},{8,0},{16,8},{24,16},{32,24},{40,32},{48,40},{56,48},{64,5... | collective-permute-start | bytes 221192 | tf_op jit(solution)/shard_map/while/body/eval_jaxpr/ppermute | solution.py:25
  384.2 3.3 convolution_add_fusion.4
  390.3 5.5 %collective-permute-start = (bf16[32,1152]{1,0:T(8,128)(2,1)S(1)}, bf16[32,1152]{1,0:T(8,128)(2,1)S(1)}, u32[]{:S(2)}, u32[]{:S(2)}) collective-permute-start(bf16[32,1152]{1,0:T(8,128)(2,1)S(1)} %copy.24), channel_id=1, source_target_pairs={{0,248},{8,0},{16,8},{24,16},{32,24},{40,32},{48,40},{56,48},{64,5... | collective-permute-start | bytes 221192 | tf_op jit(solution)/shard_map/while/body/eval_jaxpr/ppermute | solution.py:25
  396.7 3.3 convolution_add_fusion.4
  402.8 5.5 %collective-permute-start = (bf16[32,1152]{1,0:T(8,128)(2,1)S(1)}, bf16[32,1152]{1,0:T(8,128)(2,1)S(1)}, u32[]{:S(2)}, u32[]{:S(2)}) collective-permute-start(bf16[32,1152]{1,0:T(8,128)(2,1)S(1)} %copy.24), channel_id=1, source_target_pairs={{0,248},{8,0},{16,8},{24,16},{32,24},{40,32},{48,40},{56,48},{64,5... | collective-permute-start | bytes 221192 | tf_op jit(solution)/shard_map/while/body/eval_jaxpr/ppermute | solution.py:25
  409.2 3.3 convolution_add_fusion.4
  415.3 5.5 %collective-permute-start = (bf16[32,1152]{1,0:T(8,128)(2,1)S(1)}, bf16[32,1152]{1,0:T(8,128)(2,1)S(1)}, u32[]{:S(2)}, u32[]{:S(2)}) collective-permute-start(bf16[32,1152]{1,0:T(8,128)(2,1)S(1)} %copy.24), channel_id=1, source_target_pairs={{0,248},{8,0},{16,8},{24,16},{32,24},{40,32},{48,40},{56,48},{64,5... | collective-permute-start | bytes 221192 | tf_op jit(solution)/shard_map/while/body/eval_jaxpr/ppermute | solution.py:25
  421.7 3.3 convolution_add_fusion.4
  427.7 5.5 %collective-permute-start = (bf16[32,1152]{1,0:T(8,128)(2,1)S(1)}, bf16[32,1152]{1,0:T(8,128)(2,1)S(1)}, u32[]{:S(2)}, u32[]{:S(2)}) collective-permute-start(bf16[32,1152]{1,0:T(8,128)(2,1)S(1)} %copy.24), channel_id=1, source_target_pairs={{0,248},{8,0},{16,8},{24,16},{32,24},{40,32},{48,40},{56,48},{64,5... | collective-permute-start | bytes 221192 | tf_op jit(solution)/shard_map/while/body/eval_jaxpr/ppermute | solution.py:25
  440.2 5.5 %collective-permute-start = (bf16[32,1152]{1,0:T(8,128)(2,1)S(1)}, bf16[32,1152]{1,0:T(8,128)(2,1)S(1)}, u32[]{:S(2)}, u32[]{:S(2)}) collective-permute-start(bf16[32,1152]{1,0:T(8,128)(2,1)S(1)} %copy.24), channel_id=1, source_target_pairs={{0,248},{8,0},{16,8},{24,16},{32,24},{40,32},{48,40},{56,48},{64,5... | collective-permute-start | bytes 221192 | tf_op jit(solution)/shard_map/while/body/eval_jaxpr/ppermute | solution.py:25
  446.7 3.3 convolution_add_fusion.4
  452.7 5.5 %collective-permute-start = (bf16[32,1152]{1,0:T(8,128)(2,1)S(1)}, bf16[32,1152]{1,0:T(8,128)(2,1)S(1)}, u32[]{:S(2)}, u32[]{:S(2)}) collective-permute-start(bf16[32,1152]{1,0:T(8,128)(2,1)S(1)} %copy.24), channel_id=1, source_target_pairs={{0,248},{8,0},{16,8},{24,16},{32,24},{40,32},{48,40},{56,48},{64,5... | collective-permute-start | bytes 221192 | tf_op jit(solution)/shard_map/while/body/eval_jaxpr/ppermute | solution.py:25
  461.1 10.3 %collective-permute-done.2 = f32[32,1152]{1,0:T(8,128)S(1)} collective-permute-done((f32[32,1152]{1,0:T(8,128)}, f32[32,1152]{1,0:T(8,128)S(1)}, u32[]{:S(2)}, u32[]{:S(2)}) %collective-permute-start.2) | collective-permute-done | bytes 147488 | tf_op jit(solution)/shard_map/ppermute | solution.py:25
  (91 shorter events, 53.6 us)
Async XLA Ops:
  6.5 294.5 %copy-start = (bf16[1152,1152]{1,0:T(8,128)(2,1)S(1)}, bf16[1152,1152]{1,0:T(8,128)(2,1)}, u32[]{:S(2)}) copy-start(bf16[1152,1152]{1,0:T(8,128)(2,1)} %param.28) | copy-start | bytes 7962628
  6.5 256.2 %all-gather.3.cloned.1.call-start = ((), (), s32[]{:S(2)}) async-start(), calls=%async_computation.2 | async-start | bytes 11280384 | tf_op jit(solution)/shard_map/all_gather | solution.py:60
  13.1 179.6 %all-to-all-start = ((bf16[8,538,1152]{2,1,0:T(8,128)(2,1)}), bf16[8,538,1152]{2,1,0:T(8,128)(2,1)}, u32[]{:S(2)}, u32[]{:S(2)}) async-start(bf16[8,538,1152]{2,1,0:T(8,128)(2,1)} %stack.2), calls=%async_computation | async-start | bytes 20054016 | tf_op jit(solution)/shard_map/all_to_all | solution.py:69
  204.6 70.1 %copy-start.7 = (f32[4304]{0:T(1024)S(1)}, f32[4304]{0:T(1024)}, u32[]{:S(2)}) copy-start(f32[4304]{0:T(1024)} %param.23) | copy-start | bytes 51652
  204.6 70.1 %copy-start.8 = (f32[1152]{0:T(1024)S(1)}, f32[1152]{0:T(1024)}, u32[]{:S(2)}) copy-start(f32[1152]{0:T(1024)} %param.25) | copy-start | bytes 13828
  204.6 70.1 %copy-start.9 = (f32[1152]{0:T(1024)S(1)}, f32[1152]{0:T(1024)}, u32[]{:S(2)}) copy-start(f32[1152]{0:T(1024)} %param.21) | copy-start | bytes 13828
  204.6 70.1 %copy-start.10 = (f32[1152]{0:T(1024)S(1)}, f32[1152]{0:T(1024)}, u32[]{:S(2)}) copy-start(f32[1152]{0:T(1024)} %param.20) | copy-start | bytes 13828
  274.7 25.3 %copy-start.5 = (f32[1152]{0:T(1024)S(1)}, f32[1152]{0:T(1024)}, u32[]{:S(2)}) copy-start(f32[1152]{0:T(1024)} %param.26) | copy-start | bytes 13828
  302.7 16.9 %all-to-all-start.1 = ((bf16[8,32,1152]{2,1,0:T(8,128)(2,1)}), bf16[8,32,1152]{2,1,0:T(8,128)(2,1)S(1)}, u32[]{:S(2)}, u32[]{:S(2)}) async-start(bf16[8,32,1152]{2,1,0:T(8,128)(2,1)} %broadcast_in_dim.5), calls=%async_computation.1 | async-start | bytes 1179648 | tf_op jit(solution)/shard_map/all_to_all | solution.py:9
  322.9 11.4 %collective-permute-start.1 = (f32[32,1152]{1,0:T(8,128)}, f32[32,1152]{1,0:T(8,128)S(1)}, u32[]{:S(2)}, u32[]{:S(2)}) collective-permute-start(f32[32,1152]{1,0:T(8,128)} %convolution_add_fusion.4), channel_id=1, source_target_pairs={{0,248},{8,0},{16,8},{24,16},{32,24},{40,32},{48,40},{56,48},{64,5... | collective-permute-start | bytes 442376 | tf_op jit(solution)/shard_map/while/body/eval_jaxpr/ppermute | solution.py:25
  323.7 10.6 %collective-permute-start = (bf16[32,1152]{1,0:T(8,128)(2,1)S(1)}, bf16[32,1152]{1,0:T(8,128)(2,1)S(1)}, u32[]{:S(2)}, u32[]{:S(2)}) collective-permute-start(bf16[32,1152]{1,0:T(8,128)(2,1)S(1)} %copy.24), channel_id=1, source_target_pairs={{0,248},{8,0},{16,8},{24,16},{32,24},{40,32},{48,40},{56,48},{64,5... | collective-permute-start | bytes 221192 | tf_op jit(solution)/shard_map/while/body/eval_jaxpr/ppermute | solution.py:25
  337.6 9.2 %collective-permute-start.1 = (f32[32,1152]{1,0:T(8,128)}, f32[32,1152]{1,0:T(8,128)S(1)}, u32[]{:S(2)}, u32[]{:S(2)}) collective-permute-start(f32[32,1152]{1,0:T(8,128)} %convolution_add_fusion.4), channel_id=1, source_target_pairs={{0,248},{8,0},{16,8},{24,16},{32,24},{40,32},{48,40},{56,48},{64,5... | collective-permute-start | bytes 442376 | tf_op jit(solution)/shard_map/while/body/eval_jaxpr/ppermute | solution.py:25
  340.3 6.4 %collective-permute-start = (bf16[32,1152]{1,0:T(8,128)(2,1)S(1)}, bf16[32,1152]{1,0:T(8,128)(2,1)S(1)}, u32[]{:S(2)}, u32[]{:S(2)}) collective-permute-start(bf16[32,1152]{1,0:T(8,128)(2,1)S(1)} %copy.24), channel_id=1, source_target_pairs={{0,248},{8,0},{16,8},{24,16},{32,24},{40,32},{48,40},{56,48},{64,5... | collective-permute-start | bytes 221192 | tf_op jit(solution)/shard_map/while/body/eval_jaxpr/ppermute | solution.py:25
  350.1 9.2 %collective-permute-start.1 = (f32[32,1152]{1,0:T(8,128)}, f32[32,1152]{1,0:T(8,128)S(1)}, u32[]{:S(2)}, u32[]{:S(2)}) collective-permute-start(f32[32,1152]{1,0:T(8,128)} %convolution_add_fusion.4), channel_id=1, source_target_pairs={{0,248},{8,0},{16,8},{24,16},{32,24},{40,32},{48,40},{56,48},{64,5... | collective-permute-start | bytes 442376 | tf_op jit(solution)/shard_map/while/body/eval_jaxpr/ppermute | solution.py:25
  352.8 6.4 %collective-permute-start = (bf16[32,1152]{1,0:T(8,128)(2,1)S(1)}, bf16[32,1152]{1,0:T(8,128)(2,1)S(1)}, u32[]{:S(2)}, u32[]{:S(2)}) collective-permute-start(bf16[32,1152]{1,0:T(8,128)(2,1)S(1)} %copy.24), channel_id=1, source_target_pairs={{0,248},{8,0},{16,8},{24,16},{32,24},{40,32},{48,40},{56,48},{64,5... | collective-permute-start | bytes 221192 | tf_op jit(solution)/shard_map/while/body/eval_jaxpr/ppermute | solution.py:25
  362.6 9.2 %collective-permute-start.1 = (f32[32,1152]{1,0:T(8,128)}, f32[32,1152]{1,0:T(8,128)S(1)}, u32[]{:S(2)}, u32[]{:S(2)}) collective-permute-start(f32[32,1152]{1,0:T(8,128)} %convolution_add_fusion.4), channel_id=1, source_target_pairs={{0,248},{8,0},{16,8},{24,16},{32,24},{40,32},{48,40},{56,48},{64,5... | collective-permute-start | bytes 442376 | tf_op jit(solution)/shard_map/while/body/eval_jaxpr/ppermute | solution.py:25
  365.3 6.4 %collective-permute-start = (bf16[32,1152]{1,0:T(8,128)(2,1)S(1)}, bf16[32,1152]{1,0:T(8,128)(2,1)S(1)}, u32[]{:S(2)}, u32[]{:S(2)}) collective-permute-start(bf16[32,1152]{1,0:T(8,128)(2,1)S(1)} %copy.24), channel_id=1, source_target_pairs={{0,248},{8,0},{16,8},{24,16},{32,24},{40,32},{48,40},{56,48},{64,5... | collective-permute-start | bytes 221192 | tf_op jit(solution)/shard_map/while/body/eval_jaxpr/ppermute | solution.py:25
  375.0 9.2 %collective-permute-start.1 = (f32[32,1152]{1,0:T(8,128)}, f32[32,1152]{1,0:T(8,128)S(1)}, u32[]{:S(2)}, u32[]{:S(2)}) collective-permute-start(f32[32,1152]{1,0:T(8,128)} %convolution_add_fusion.4), channel_id=1, source_target_pairs={{0,248},{8,0},{16,8},{24,16},{32,24},{40,32},{48,40},{56,48},{64,5... | collective-permute-start | bytes 442376 | tf_op jit(solution)/shard_map/while/body/eval_jaxpr/ppermute | solution.py:25
  377.8 6.4 %collective-permute-start = (bf16[32,1152]{1,0:T(8,128)(2,1)S(1)}, bf16[32,1152]{1,0:T(8,128)(2,1)S(1)}, u32[]{:S(2)}, u32[]{:S(2)}) collective-permute-start(bf16[32,1152]{1,0:T(8,128)(2,1)S(1)} %copy.24), channel_id=1, source_target_pairs={{0,248},{8,0},{16,8},{24,16},{32,24},{40,32},{48,40},{56,48},{64,5... | collective-permute-start | bytes 221192 | tf_op jit(solution)/shard_map/while/body/eval_jaxpr/ppermute | solution.py:25
  387.5 9.2 %collective-permute-start.1 = (f32[32,1152]{1,0:T(8,128)}, f32[32,1152]{1,0:T(8,128)S(1)}, u32[]{:S(2)}, u32[]{:S(2)}) collective-permute-start(f32[32,1152]{1,0:T(8,128)} %convolution_add_fusion.4), channel_id=1, source_target_pairs={{0,248},{8,0},{16,8},{24,16},{32,24},{40,32},{48,40},{56,48},{64,5... | collective-permute-start | bytes 442376 | tf_op jit(solution)/shard_map/while/body/eval_jaxpr/ppermute | solution.py:25
  390.3 6.4 %collective-permute-start = (bf16[32,1152]{1,0:T(8,128)(2,1)S(1)}, bf16[32,1152]{1,0:T(8,128)(2,1)S(1)}, u32[]{:S(2)}, u32[]{:S(2)}) collective-permute-start(bf16[32,1152]{1,0:T(8,128)(2,1)S(1)} %copy.24), channel_id=1, source_target_pairs={{0,248},{8,0},{16,8},{24,16},{32,24},{40,32},{48,40},{56,48},{64,5... | collective-permute-start | bytes 221192 | tf_op jit(solution)/shard_map/while/body/eval_jaxpr/ppermute | solution.py:25
  400.0 9.2 %collective-permute-start.1 = (f32[32,1152]{1,0:T(8,128)}, f32[32,1152]{1,0:T(8,128)S(1)}, u32[]{:S(2)}, u32[]{:S(2)}) collective-permute-start(f32[32,1152]{1,0:T(8,128)} %convolution_add_fusion.4), channel_id=1, source_target_pairs={{0,248},{8,0},{16,8},{24,16},{32,24},{40,32},{48,40},{56,48},{64,5... | collective-permute-start | bytes 442376 | tf_op jit(solution)/shard_map/while/body/eval_jaxpr/ppermute | solution.py:25
  402.8 6.4 %collective-permute-start = (bf16[32,1152]{1,0:T(8,128)(2,1)S(1)}, bf16[32,1152]{1,0:T(8,128)(2,1)S(1)}, u32[]{:S(2)}, u32[]{:S(2)}) collective-permute-start(bf16[32,1152]{1,0:T(8,128)(2,1)S(1)} %copy.24), channel_id=1, source_target_pairs={{0,248},{8,0},{16,8},{24,16},{32,24},{40,32},{48,40},{56,48},{64,5... | collective-permute-start | bytes 221192 | tf_op jit(solution)/shard_map/while/body/eval_jaxpr/ppermute | solution.py:25
  412.5 9.2 %collective-permute-start.1 = (f32[32,1152]{1,0:T(8,128)}, f32[32,1152]{1,0:T(8,128)S(1)}, u32[]{:S(2)}, u32[]{:S(2)}) collective-permute-start(f32[32,1152]{1,0:T(8,128)} %convolution_add_fusion.4), channel_id=1, source_target_pairs={{0,248},{8,0},{16,8},{24,16},{32,24},{40,32},{48,40},{56,48},{64,5... | collective-permute-start | bytes 442376 | tf_op jit(solution)/shard_map/while/body/eval_jaxpr/ppermute | solution.py:25
  415.3 6.4 %collective-permute-start = (bf16[32,1152]{1,0:T(8,128)(2,1)S(1)}, bf16[32,1152]{1,0:T(8,128)(2,1)S(1)}, u32[]{:S(2)}, u32[]{:S(2)}) collective-permute-start(bf16[32,1152]{1,0:T(8,128)(2,1)S(1)} %copy.24), channel_id=1, source_target_pairs={{0,248},{8,0},{16,8},{24,16},{32,24},{40,32},{48,40},{56,48},{64,5... | collective-permute-start | bytes 221192 | tf_op jit(solution)/shard_map/while/body/eval_jaxpr/ppermute | solution.py:25
  425.0 9.2 %collective-permute-start.1 = (f32[32,1152]{1,0:T(8,128)}, f32[32,1152]{1,0:T(8,128)S(1)}, u32[]{:S(2)}, u32[]{:S(2)}) collective-permute-start(f32[32,1152]{1,0:T(8,128)} %convolution_add_fusion.4), channel_id=1, source_target_pairs={{0,248},{8,0},{16,8},{24,16},{32,24},{40,32},{48,40},{56,48},{64,5... | collective-permute-start | bytes 442376 | tf_op jit(solution)/shard_map/while/body/eval_jaxpr/ppermute | solution.py:25
  427.7 6.4 %collective-permute-start = (bf16[32,1152]{1,0:T(8,128)(2,1)S(1)}, bf16[32,1152]{1,0:T(8,128)(2,1)S(1)}, u32[]{:S(2)}, u32[]{:S(2)}) collective-permute-start(bf16[32,1152]{1,0:T(8,128)(2,1)S(1)} %copy.24), channel_id=1, source_target_pairs={{0,248},{8,0},{16,8},{24,16},{32,24},{40,32},{48,40},{56,48},{64,5... | collective-permute-start | bytes 221192 | tf_op jit(solution)/shard_map/while/body/eval_jaxpr/ppermute | solution.py:25
  437.5 9.2 %collective-permute-start.1 = (f32[32,1152]{1,0:T(8,128)}, f32[32,1152]{1,0:T(8,128)S(1)}, u32[]{:S(2)}, u32[]{:S(2)}) collective-permute-start(f32[32,1152]{1,0:T(8,128)} %convolution_add_fusion.4), channel_id=1, source_target_pairs={{0,248},{8,0},{16,8},{24,16},{32,24},{40,32},{48,40},{56,48},{64,5... | collective-permute-start | bytes 442376 | tf_op jit(solution)/shard_map/while/body/eval_jaxpr/ppermute | solution.py:25
  440.2 6.4 %collective-permute-start = (bf16[32,1152]{1,0:T(8,128)(2,1)S(1)}, bf16[32,1152]{1,0:T(8,128)(2,1)S(1)}, u32[]{:S(2)}, u32[]{:S(2)}) collective-permute-start(bf16[32,1152]{1,0:T(8,128)(2,1)S(1)} %copy.24), channel_id=1, source_target_pairs={{0,248},{8,0},{16,8},{24,16},{32,24},{40,32},{48,40},{56,48},{64,5... | collective-permute-start | bytes 221192 | tf_op jit(solution)/shard_map/while/body/eval_jaxpr/ppermute | solution.py:25
  450.0 9.2 %collective-permute-start.1 = (f32[32,1152]{1,0:T(8,128)}, f32[32,1152]{1,0:T(8,128)S(1)}, u32[]{:S(2)}, u32[]{:S(2)}) collective-permute-start(f32[32,1152]{1,0:T(8,128)} %convolution_add_fusion.4), channel_id=1, source_target_pairs={{0,248},{8,0},{16,8},{24,16},{32,24},{40,32},{48,40},{56,48},{64,5... | collective-permute-start | bytes 442376 | tf_op jit(solution)/shard_map/while/body/eval_jaxpr/ppermute | solution.py:25
  452.7 6.4 %collective-permute-start = (bf16[32,1152]{1,0:T(8,128)(2,1)S(1)}, bf16[32,1152]{1,0:T(8,128)(2,1)S(1)}, u32[]{:S(2)}, u32[]{:S(2)}) collective-permute-start(bf16[32,1152]{1,0:T(8,128)(2,1)S(1)} %copy.24), channel_id=1, source_target_pairs={{0,248},{8,0},{16,8},{24,16},{32,24},{40,32},{48,40},{56,48},{64,5... | collective-permute-start | bytes 221192 | tf_op jit(solution)/shard_map/while/body/eval_jaxpr/ppermute | solution.py:25
  461.1 10.3 %collective-permute-start.2 = (f32[32,1152]{1,0:T(8,128)}, f32[32,1152]{1,0:T(8,128)S(1)}, u32[]{:S(2)}, u32[]{:S(2)}) collective-permute-start(f32[32,1152]{1,0:T(8,128)} %convolution_add_fusion.1), channel_id=1, source_target_pairs={{0,88},{8,96},{16,104},{24,112},{32,120},{40,128},{48,136},{56,144... | collective-permute-start | bytes 442376 | tf_op jit(solution)/shard_map/ppermute | solution.py:25
  (5 other events, 20.1 us)
Sparse Core Ops, SparseCore 0:
  9.1 253.5 all-gather.2
